TPU v7x, 32 devices: a whole 2x2x4 slice. The times are simulated.
32 devices in a mesh: ctx: 8 (over z, x), bit: 4 (over y, core).
Axes of the slice: x: 2, y: 2, z: 4, core: 2. Of those that a mesh axis runs over, the one named last changes fastest.
Arguments:
- query_proj: bfloat16 [4096, 4096], P(None, ('ctx', 'bit')), may hold values from -6 to 6
- key_proj: bfloat16 [4096, 4096], P(None, ('ctx', 'bit')), may hold values from -6 to 6
- value_proj: bfloat16 [4096, 4096], P(None, ('ctx', 'bit')), may hold values from -6 to 6
- filter_taps: bfloat16 [4096, 4096], P(None, ('ctx', 'bit')), may hold values from -0.09375 to 0.09375
- skip_gain: float32 [4096], replicated, may hold values from -4 to 4
Outputs:
- gated: bfloat16 [4096, 4096], P(None, ('ctx', 'bit'))
All inputs are finite; a program needn't handle non-finite values.
Results may differ from a plain program's by a relative error of at most 0.0049.
Values may be sent and summed in bfloat16 or wider, within the bound.
No kernel may reach another device: no remote copies, remote signals or barrier semaphores. Data moves between devices by JAX's collectives and lax.ppermute only.
A program may use at most 128 MiB of HBM per device.

v0:
```python
import functools
import math

import jax
import jax.numpy as jnp
import ml_dtypes
import numpy as np
from jax import lax
from jax.experimental import pallas as pl
from jax.experimental.pallas import tpu as pltpu
from jax.sharding import PartitionSpec as P

BLOCKS, LANES, TOTAL = 32, 128, 8192
ROOT_HALF = math.sqrt(0.5)
COS8, SIN8 = math.cos(math.pi / 8), math.sin(math.pi / 8)


def split_table(table):
    high = table.astype(ml_dtypes.bfloat16)
    low = (table - high.astype(np.float64)).astype(ml_dtypes.bfloat16)
    return np.concatenate([high, high, low], axis=0)


@functools.lru_cache(None)
def tables():
    j = np.arange(LANES)
    angle = 2 * np.pi * (j[:, None] * j[None, :] % LANES) / LANES
    c, s = np.cos(angle), np.sin(angle)
    to_freq = split_table(np.block([[c, -s], [s, c]]))
    to_time = split_table(np.block([[c, s], [-s, c]]))
    m = (np.arange(4)[:, None] + 4 * np.arange(8)[None, :]).reshape(-1)
    twist = 2 * np.pi * ((4 * m + 1)[:, None] * j[None, :] % (2 * TOTAL)) / (2 * TOTAL)
    twist_in = np.stack([np.cos(twist), -np.sin(twist)], 1).astype(np.float32)
    twist_out = (2.0 / TOTAL * np.stack([np.cos(twist), np.sin(twist)], 1)).astype(np.float32)
    return to_freq, to_time, twist_in, twist_out


def cadd(a, b):
    return (a[0] + b[0], a[1] + b[1])


def csub(a, b):
    return (a[0] - b[0], a[1] - b[1])


def turn(a, numer, denom):
    if numer == 0:
        return a
    c, s = math.cos(math.pi * numer / denom), math.sin(math.pi * numer / denom)
    return (a[0] * c - a[1] * s, a[0] * s + a[1] * c)


def times_i(a, sign):
    return (-a[1], a[0]) if sign > 0 else (a[1], -a[0])


def dft4(x, sign):
    a, b, c, d = cadd(x[0], x[2]), csub(x[0], x[2]), cadd(x[1], x[3]), csub(x[1], x[3])
    if sign > 0:
        return [cadd(a, c), (b[0] - d[1], b[1] + d[0]), csub(a, c), (b[0] + d[1], b[1] - d[0])]
    return [cadd(a, c), (b[0] + d[1], b[1] - d[0]), csub(a, c), (b[0] - d[1], b[1] + d[0])]


def dft8(x, sign):
    e, o = dft4(x[0::2], sign), dft4(x[1::2], sign)
    p, q = o[1], o[3]
    if sign > 0:
        o1 = ((p[0] - p[1]) * ROOT_HALF, (p[0] + p[1]) * ROOT_HALF)
        o3 = ((q[0] + q[1]) * ROOT_HALF, (q[1] - q[0]) * ROOT_HALF)
        two = [(e[2][0] - o[2][1], e[2][1] + o[2][0]), (e[2][0] + o[2][1], e[2][1] - o[2][0])]
        three = [(e[3][0] - o3[0], e[3][1] - o3[1]), (e[3][0] + o3[0], e[3][1] + o3[1])]
    else:
        o1 = ((p[0] + p[1]) * ROOT_HALF, (p[1] - p[0]) * ROOT_HALF)
        o3 = ((q[0] - q[1]) * ROOT_HALF, (q[0] + q[1]) * ROOT_HALF)
        two = [(e[2][0] + o[2][1], e[2][1] - o[2][0]), (e[2][0] - o[2][1], e[2][1] + o[2][0])]
        three = [(e[3][0] - o3[0], e[3][1] - o3[1]), (e[3][0] + o3[0], e[3][1] + o3[1])]
    return [cadd(e[0], o[0]), cadd(e[1], o1), two[0], three[0], csub(e[0], o[0]), csub(e[1], o1), two[1], three[1]]


def first_stage(load, stage, group):
    for n2 in range(8):
        a0, a1, a2, a3 = [load(8 * n1 + n2) for n1 in range(4)]
        r = a2 * ROOT_HALF
        c1, s1, c3, s3 = a1 * COS8, a1 * SIN8, a3 * SIN8, a3 * COS8
        ar, br = a0 + r, a0 - r
        cr, ci, dr, di = c1 + c3, s1 + s3, c1 - c3, s3 - s1
        outs = [(ar + cr, -r - ci), (br + di, r - dr), (ar - cr, ci - r), (br - di, r + dr)]
        for m1 in range(4):
            put_row(stage, 8 * m1 + n2, group, turn(outs[m1], -n2 * (1 + 4 * m1), 64))


def put_row(dest, row, group, value):
    dest[row * group : (row + 1) * group, :LANES] = value[0]
    dest[row * group : (row + 1) * group, LANES:] = value[1]


def split(x):
    high = x.astype(jnp.bfloat16)
    return high, (x - high.astype(jnp.float32)).astype(jnp.bfloat16)


def put_split(dest, row, group, re, im):
    for at, part in ((0, re), (LANES, im)):
        high, low = split(part)
        dest[row * group : (row + 1) * group, at : at + LANES] = high
        dest[row * group : (row + 1) * group, 2 * LANES + at : 3 * LANES + at] = low


def twisted(values, m1, twist_ref):
    out = []
    for m2, (re, im) in enumerate(values):
        c, s = twist_ref[8 * m1 + m2, 0:1, :], twist_ref[8 * m1 + m2, 1:2, :]
        out.append((re * c - im * s, re * s + im * c))
    return out


def put_chunk(dest, m1, group, values):
    for m2, (re, im) in enumerate(values):
        put_split(dest, 8 * m1 + m2, group, re, im)


def apply_table(source, table_ref, dest, m1, group):
    rows = slice(8 * m1 * group, 8 * (m1 + 1) * group)
    high, low = source[rows, : 2 * LANES], source[rows, 2 * LANES :]
    dest[rows, :] = jnp.dot(
        jnp.concatenate([high, low, high], axis=1), table_ref[...], preferred_element_type=jnp.float32
    )


def get_chunk(source, m1, group):
    out = []
    for m2 in range(8):
        rows = slice((8 * m1 + m2) * group, (8 * m1 + m2 + 1) * group)
        out.append((source[rows, :LANES], source[rows, LANES:]))
    return out


def get_row(source, row, group):
    rows = slice(row * group, (row + 1) * group)
    return (source[rows, :LANES], source[rows, LANES:])


def last_stage(stage, skip, load, store, group):
    for n2 in range(8):
        v = [turn(get_row(stage, 8 * m1 + n2, group), n2 * (1 + 4 * m1), 64) for m1 in range(4)]
        a, b, c, d = cadd(v[0], v[2]), csub(v[0], v[2]), cadd(v[1], v[3]), csub(v[1], v[3])
        outs = [
            a[0] + c[0],
            (b[0] - d[1]) * COS8 - (b[1] + d[0]) * SIN8,
            ((a[0] - c[0]) - (a[1] - c[1])) * ROOT_HALF,
            (b[0] + d[1]) * SIN8 - (b[1] - d[0]) * COS8,
        ]
        for n1 in range(4):
            n = 8 * n1 + n2
            store(n, outs[n1] + skip * load(n))


def conv_kernel(r_ref, skip_ref, freq_ref, time_ref, tin_ref, tout_ref, o_ref, ta, pa, xa, tf, pf, xf, ts, ps, xs, group, ch):
    def body(g, carry):
        at = pl.multiple_of(g * group, group)
        mine = pl.ds(at, group)
        prods = pl.ds(pl.multiple_of(ch + at, group), group)

        def load_taps(n):
            return r_ref[n, mine, :].astype(jnp.float32)

        def load_prods(n):
            return r_ref[n, prods, :].astype(jnp.float32)

        def store(n, value):
            o_ref[n, mine, :] = value.astype(o_ref.dtype)

        first_stage(load_taps, ts, group)
        first_stage(load_prods, ps, group)

        def fwd(m1):
            put_chunk(ta, m1, group, twisted(dft8(get_chunk(ts, m1, group), -1), m1, tin_ref))
            apply_table(ta, freq_ref, tf, m1, group)
            put_chunk(pa, m1, group, twisted(dft8(get_chunk(ps, m1, group), -1), m1, tin_ref))
            apply_table(pa, freq_ref, pf, m1, group)

        def mid(m1):
            pairs = zip(get_chunk(tf, m1, group), get_chunk(pf, m1, group))
            put_chunk(xa, m1, group, [(a * c - b * d, a * d + b * c) for (a, b), (c, d) in pairs])
            apply_table(xa, time_ref, xf, m1, group)

        def bwd(m1):
            for m2, value in enumerate(dft8(twisted(get_chunk(xf, m1, group), m1, tout_ref), 1)):
                put_row(xs, 8 * m1 + m2, group, value)

        for step in range(6):
            if step < 4:
                fwd(step)
            if 0 <= step - 1 < 4:
                mid(step - 1)
            if 0 <= step - 2 < 4:
                bwd(step - 2)
        lane = lax.broadcasted_iota(jnp.int32, (group, ch), 1) - lax.broadcasted_iota(jnp.int32, (group, ch), 0)
        skip = jnp.sum(jnp.where(lane == at, skip_ref[...], 0.0), axis=1, keepdims=True)
        last_stage(xs, skip, load_prods, store, group)
        return carry

    lax.fori_loop(0, ch // group, body, 0)


def conv_call(recv, skip, group=16, interpret=False):
    blocks, rows, length = recv.shape
    ch = rows // 2
    whole = pl.BlockSpec(memory_space=pltpu.VMEM)
    return pl.pallas_call(
        functools.partial(conv_kernel, group=group, ch=ch),
        out_shape=jax.ShapeDtypeStruct((blocks, ch, length), jnp.bfloat16),
        in_specs=[whole] * 6,
        out_specs=whole,
        scratch_shapes=[pltpu.VMEM((BLOCKS * group, 4 * LANES), jnp.bfloat16)] * 3
        + [pltpu.VMEM((BLOCKS * group, 2 * LANES), jnp.float32)] * 6,
        compiler_params=pltpu.CompilerParams(vmem_limit_bytes=14 << 20),
        cost_estimate=pl.CostEstimate(
            flops=36 * BLOCKS * ch * 256 * 256, bytes_accessed=6 * BLOCKS * ch * LANES, transcendentals=0
        ),
        interpret=interpret,
    )(recv, skip, *[jnp.asarray(table) for table in tables()])


EXACT_MODE = lax.Precision.HIGHEST
FULL_TURN = 2.0 * math.pi


def rotation(left_index, right_index, length, orient):
    phases = left_index[:, None] * right_index[None, :] % length
    angles = orient * FULL_TURN / length * phases.astype(jnp.float32)
    return (jnp.cos(angles), jnp.sin(angles))


def contract(form, data, table):
    return jnp.einsum(form, data, table, precision=EXACT_MODE, preferred_element_type=jnp.float32)


def apply_rotation(form, real_part, imag_part, cos_table, sin_table):
    out_real = contract(form, real_part, cos_table) - contract(form, imag_part, sin_table)
    out_imag = contract(form, real_part, sin_table) + contract(form, imag_part, cos_table)
    return (out_real, out_imag)


def complex_times(a_real, a_imag, b_real, b_imag):
    return (a_real * b_real - a_imag * b_imag, a_real * b_imag + a_imag * b_real)


def conv_general(recv, skip):
    blocks, rows, length = recv.shape
    ch = rows // 2
    rows_fft = 2 * blocks
    total_len = rows_fft * length
    stacked = jnp.stack([recv[:, ch:], recv[:, :ch]]).astype(jnp.float32)
    positions = jnp.arange(length, dtype=jnp.int32)
    natural_rows = jnp.arange(rows_fft, dtype=jnp.int32)
    block_index = jnp.arange(blocks, dtype=jnp.int32)
    cos_fwd, sin_fwd = rotation(natural_rows, block_index, rows_fft, -1.0)
    spec_real = contract("gjcp,rj->grcp", stacked, cos_fwd)
    spec_imag = contract("gjcp,rj->grcp", stacked, sin_fwd)
    twist_cos, twist_sin = rotation(natural_rows, positions, total_len, -1.0)
    spec_real, spec_imag = complex_times(spec_real, spec_imag, twist_cos[None, :, None, :], twist_sin[None, :, None, :])
    low_cos, low_sin = rotation(positions, positions, length, -1.0)
    spec_real, spec_imag = apply_rotation("...p,pk->...k", spec_real, spec_imag, low_cos, low_sin)
    out_real, out_imag = complex_times(spec_real[0], spec_imag[0], spec_real[1], spec_imag[1])
    out_real, out_imag = apply_rotation("...k,pk->...p", out_real, out_imag, low_cos, -low_sin)
    out_real, out_imag = complex_times(out_real, out_imag, twist_cos[:, None, :], -twist_sin[:, None, :])
    inv_cos, inv_sin = rotation(block_index, natural_rows, rows_fft, 1.0)
    conv = (contract("rcp,jr->jcp", out_real, inv_cos) - contract("rcp,jr->jcp", out_imag, inv_sin)) / total_len
    return (conv + skip * stacked[0]).astype(jnp.bfloat16)


def on_device(query_proj, key_proj, value_proj, filter_taps, skip_gain):
    channels, length = query_proj.shape
    axes = ("ctx", "bit")
    devices_all = lax.axis_size("ctx") * lax.axis_size("bit")
    ch_dev = channels // devices_all
    products = key_proj * value_proj
    send = jnp.concatenate(
        [filter_taps.reshape(devices_all, ch_dev, length), products.reshape(devices_all, ch_dev, length)], axis=1
    )
    mine = lax.axis_index(axes)
    skip = lax.dynamic_slice(skip_gain, (mine * ch_dev,), (ch_dev,))[None, :]
    send, skip = lax.optimization_barrier((send, skip))
    recv = lax.all_to_all(send, axes, split_axis=0, concat_axis=0, tiled=True)
    if devices_all == 32 and length == 128 and ch_dev % 16 == 0:
        mixed = conv_call(recv, skip)
    else:
        mixed = conv_general(recv, skip.reshape(ch_dev, 1))
    home = lax.all_to_all(mixed, axes, split_axis=0, concat_axis=0, tiled=True).reshape(channels, length)
    return (query_proj.astype(jnp.float32) * home.astype(jnp.float32)).astype(jnp.bfloat16)


def solution(mesh):
    placed = (P(None, ("ctx", "bit")),) * 4 + (P(),)
    return jax.shard_map(
        on_device, mesh=mesh, in_specs=placed, out_specs=P(None, ("ctx", "bit")), check_vma=False
    )
```

profile of v0, /device:TPU:0, one launch (start us, length us, event | category | flops | bytes accessed | tf_op | source)
XLA Modules:
  0.0 101.3 jit_solution(14471575566878370222)
XLA Ops:
  0.0 0.0 copy-start
  0.0 0.0 copy-start.6
  0.0 0.7 copy-done
  0.7 0.1 dynamic-slice_bitcast_fusion.skip_ref
  0.8 1.8 %mul.12 = bf16[4096,128]{1,0:T(8,128)(2,1)S(1)} multiply(bf16[4096,128]{1,0:T(8,128)(2,1)} %param.10, bf16[4096,128]{1,0:T(8,128)(2,1)} %param.11) | non-fusion elementwise | flops 524288 | bytes 3145728 | tf_op jit(solution)/shard_map/mul | solution.py:278
  2.6 0.0 copy-done.6
  2.6 0.2 pad_maximum_fusion
  2.8 0.0 copy-start.1
  2.8 0.0 copy-start.2
  2.8 0.0 copy-start.3
  2.8 0.0 copy-start.4
  2.9 55.8 %all_to_all.10.r_ref = bf16[32,256,128]{2,1,0:T(8,128)(2,1)S(1)} all-to-all(bf16[32,256,128]{2,1,0:T(8,128)(2,1)S(1)} %pad_maximum_fusion), channel_id=1, replica_groups=mesh['ctx'=8,'bit'=4] {'ctx','bit'}, dimensions={0} | all-to-all | bytes 4194304 | tf_op jit(solution)/shard_map/all_to_all | solution.py:285
  58.7 0.0 copy-done.1
  58.7 0.0 copy-done.2
  58.7 0.0 copy-done.3
  58.7 0.0 copy-done.4
  58.7 11.6 %shard_map.91 = bf16[32,128,128]{2,1,0:T(8,128)(2,1)S(1)} custom-call(bf16[32,256,128]{2,1,0:T(8,128)(2,1)S(1)} %all_to_all.10.r_ref, f32[1,128]{1,0:T(1,128)S(1)} %dynamic-slice_bitcast_fusion.skip_ref, bf16[768,256]{1,0:T(8,128)(2,1)S(1)} %copy-done.2, bf16[768,256]{1,0:T(8,128)(2,1)S(1)} %copy-done.1, f32[32,2,128]{2,1,0:T(2,128)S(1)} %copy-done.4, ...), custom_call_target="tpu_custom_call" | custom-call | flops 9663676416 | bytes 3145728 | tf_op jit(solution)/shard_map/pallas_call | solution.py:210
  70.3 0.0 copy-start.5
  70.3 29.7 %all_to_all.11 = bf16[32,128,128]{2,1,0:T(8,128)(2,1)S(1)} all-to-all(bf16[32,128,128]{2,1,0:T(8,128)(2,1)S(1)} %shard_map.91), channel_id=1, replica_groups=mesh['ctx'=8,'bit'=4] {'ctx','bit'}, dimensions={0} | all-to-all | bytes 2097152 | tf_op jit(solution)/shard_map/all_to_all | solution.py:290
  100.0 0.0 copy-done.5
  100.0 1.3 %fusion = bf16[4096,128]{1,0:T(8,128)(2,1)} fusion(bf16[4096,128]{1,0:T(8,128)(2,1)S(1)} %copy-done.5, bf16[32,128,128]{2,1,0:T(8,128)(2,1)S(1)} %all_to_all.11), kind=kLoop, calls=%fused_computation.2 | loop fusion | flops 2097152 | bytes 3145728 | tf_op jit(solution)/shard_map/convert_element_type | solution.py:291
Async XLA Ops:
  0.0 0.7 copy-start
  0.0 2.6 %copy-start.6 = (bf16[4096,128]{1,0:T(8,128)(2,1)S(1)}, bf16[4096,128]{1,0:T(8,128)(2,1)}, u32[]{:S(2)}) copy-start(bf16[4096,128]{1,0:T(8,128)(2,1)} %param.12) | copy-start | bytes 3145732
  2.8 55.9 %copy-start.1 = (bf16[768,256]{1,0:T(8,128)(2,1)S(1)}, bf16[768,256]{1,0:T(8,128)(2,1)}, u32[]{:S(2)}) copy-start(bf16[768,256]{1,0:T(8,128)(2,1)} %constant.26.clone.time_ref) | copy-start | bytes 1179652
  2.8 55.9 %copy-start.2 = (bf16[768,256]{1,0:T(8,128)(2,1)S(1)}, bf16[768,256]{1,0:T(8,128)(2,1)}, u32[]{:S(2)}) copy-start(bf16[768,256]{1,0:T(8,128)(2,1)} %constant.25.clone.freq_ref) | copy-start | bytes 1179652
  2.8 55.8 %copy-start.3 = (f32[32,2,128]{2,1,0:T(2,128)S(1)}, f32[32,2,128]{2,1,0:T(2,128)}, u32[]{:S(2)}) copy-start(f32[32,2,128]{2,1,0:T(2,128)} %constant.28.clone.tout_ref) | copy-start | bytes 98308
  2.8 55.8 %copy-start.4 = (f32[32,2,128]{2,1,0:T(2,128)S(1)}, f32[32,2,128]{2,1,0:T(2,128)}, u32[]{:S(2)}) copy-start(f32[32,2,128]{2,1,0:T(2,128)} %constant.27.clone.tin_ref) | copy-start | bytes 98308
  70.3 29.7 %copy-start.5 = (bf16[4096,128]{1,0:T(8,128)(2,1)S(1)}, bf16[4096,128]{1,0:T(8,128)(2,1)}, u32[]{:S(2)}) copy-start(bf16[4096,128]{1,0:T(8,128)(2,1)} %param.9) | copy-start | bytes 3145732
where the time goes:
time: 102 us; the launch traced here: 101 us
  blocking collectives  85.5 us (84%)
  Pallas kernels  11.6 us (11%)
  other arithmetic  3.3 us (3%)
    all_to_all x1, blocking collectives, on_device(): recv = lax.all_to_all(send, axes, split_axis=0, concat_axis=0, tiled=True)  55.8 us
    all_to_all x1, blocking collectives, on_device(): lax.all_to_all(mixed, axes, split_axis=0, concat_axis=0, tiled=True)  29.7 us
    pallas_call x1, Pallas kernels, conv_call(): pl.pallas_call(functools.partial(conv_kernel, group=group, ch=ch), out_sh...  11.6 us

commit v1 on v0

--- a/solution.py
+++ b/solution.py
@@ -1,4 +1,5 @@
 import functools
+import itertools
 import math
 
 import jax
@@ -155,32 +156,37 @@
             store(n, outs[n1] + skip * load(n))
 
 
-def conv_kernel(r_ref, skip_ref, freq_ref, time_ref, tin_ref, tout_ref, o_ref, ta, pa, xa, tf, pf, xf, ts, ps, xs, group, ch):
-    def body(g, carry):
-        at = pl.multiple_of(g * group, group)
-        mine = pl.ds(at, group)
-        prods = pl.ds(pl.multiple_of(ch + at, group), group)
-
-        def load_taps(n):
-            return r_ref[n, mine, :].astype(jnp.float32)
-
-        def load_prods(n):
-            return r_ref[n, prods, :].astype(jnp.float32)
-
+def conv_kernel(r_ref, skip_ref, freq_ref, time_ref, tin_ref, tout_ref, o_ref, *scratch, group, ch):
+    ta, pa, xa, xf, ts, ps, xs = scratch[:7]
+    tf, pf = scratch[7:9], scratch[9:11]
+    steps = ch // group
+
+    def rows(g, base=0):
+        return slice(base + g * group, base + (g + 1) * group)
+
+    def loader(g, base):
+        return lambda n: r_ref[n, rows(g, base), :].astype(jnp.float32)
+
+    def storer(g):
         def store(n, value):
-            o_ref[n, mine, :] = value.astype(o_ref.dtype)
-
-        first_stage(load_taps, ts, group)
-        first_stage(load_prods, ps, group)
-
-        def fwd(m1):
-            put_chunk(ta, m1, group, twisted(dft8(get_chunk(ts, m1, group), -1), m1, tin_ref))
-            apply_table(ta, freq_ref, tf, m1, group)
-            put_chunk(pa, m1, group, twisted(dft8(get_chunk(ps, m1, group), -1), m1, tin_ref))
-            apply_table(pa, freq_ref, pf, m1, group)
-
+            o_ref[n, rows(g), :] = value.astype(o_ref.dtype)
+
+        return store
+
+    def head(g):
+        def fwd(stage, a, f, m1):
+            put_chunk(a, m1, group, twisted(dft8(get_chunk(stage, m1, group), -1), m1, tin_ref))
+            apply_table(a, freq_ref, f, m1, group)
+
+        yield lambda: first_stage(loader(g, 0), ts, group)
+        yield lambda: first_stage(loader(g, ch), ps, group)
+        for m1 in range(4):
+            yield lambda: fwd(ts, ta, tf[g % 2], m1)
+            yield lambda: fwd(ps, pa, pf[g % 2], m1)
+
+    def tail(g):
         def mid(m1):
-            pairs = zip(get_chunk(tf, m1, group), get_chunk(pf, m1, group))
+            pairs = zip(get_chunk(tf[g % 2], m1, group), get_chunk(pf[g % 2], m1, group))
             put_chunk(xa, m1, group, [(a * c - b * d, a * d + b * c) for (a, b), (c, d) in pairs])
             apply_table(xa, time_ref, xf, m1, group)
 
@@ -188,19 +194,28 @@
             for m2, value in enumerate(dft8(twisted(get_chunk(xf, m1, group), m1, tout_ref), 1)):
                 put_row(xs, 8 * m1 + m2, group, value)
 
-        for step in range(6):
-            if step < 4:
-                fwd(step)
-            if 0 <= step - 1 < 4:
-                mid(step - 1)
-            if 0 <= step - 2 < 4:
-                bwd(step - 2)
-        lane = lax.broadcasted_iota(jnp.int32, (group, ch), 1) - lax.broadcasted_iota(jnp.int32, (group, ch), 0)
-        skip = jnp.sum(jnp.where(lane == at, skip_ref[...], 0.0), axis=1, keepdims=True)
-        last_stage(xs, skip, load_prods, store, group)
-        return carry
-
-    lax.fori_loop(0, ch // group, body, 0)
+        def last():
+            lane = lax.broadcasted_iota(jnp.int32, (group, ch), 1) - lax.broadcasted_iota(jnp.int32, (group, ch), 0)
+            skip = jnp.sum(jnp.where(lane == g * group, skip_ref[...], 0.0), axis=1, keepdims=True)
+            last_stage(xs, skip, loader(g, ch), storer(g), group)
+
+        yield lambda: mid(0)
+        yield lambda: mid(1)
+        yield lambda: mid(2)
+        yield lambda: bwd(0)
+        yield lambda: mid(3)
+        yield lambda: bwd(1)
+        yield lambda: bwd(2)
+        yield lambda: bwd(3)
+        yield last
+
+    for g in range(steps + 1):
+        streams = [tail(g - 1)] if g > 0 else []
+        streams += [head(g)] if g < steps else []
+        for now in itertools.zip_longest(*streams):
+            for piece in now:
+                if piece is not None:
+                    piece()
 
 
 def conv_call(recv, skip, group=16, interpret=False):
@@ -213,7 +228,7 @@
         in_specs=[whole] * 6,
         out_specs=whole,
         scratch_shapes=[pltpu.VMEM((BLOCKS * group, 4 * LANES), jnp.bfloat16)] * 3
-        + [pltpu.VMEM((BLOCKS * group, 2 * LANES), jnp.float32)] * 6,
+        + [pltpu.VMEM((BLOCKS * group, 2 * LANES), jnp.float32)] * 8,
         compiler_params=pltpu.CompilerParams(vmem_limit_bytes=14 << 20),
         cost_estimate=pl.CostEstimate(
             flops=36 * BLOCKS * ch * 256 * 256, bytes_accessed=6 * BLOCKS * ch * LANES, transcendentals=0

time: 102 us -> 101 us (level)
  no operation moved by 1% of the time
where the time goes in v1:
time: 101 us
  blocking collectives  85.5 us (85%)
  Pallas kernels  10.8 us (11%)
  other arithmetic  3.3 us (3%)
    all_to_all x1, blocking collectives, on_device(): recv = lax.all_to_all(send, axes, split_axis=0, concat_axis=0, tiled=True)  55.8 us
    all_to_all x1, blocking collectives, on_device(): lax.all_to_all(mixed, axes, split_axis=0, concat_axis=0, tiled=True)  29.7 us
    pallas_call x1, Pallas kernels, conv_call(): pl.pallas_call(functools.partial(conv_kernel, group=group, ch=ch), out_sh...  10.8 us

profile of v1, /device:TPU:0, one launch (start us, length us, event | category | flops | bytes accessed | tf_op | source)
XLA Modules:
  0.0 100.5 jit_solution(4714458438328822563)
XLA Ops:
  0.0 0.0 copy-start
  0.0 0.0 copy-start.6
  0.0 0.7 copy-done
  0.7 0.1 dynamic-slice_bitcast_fusion.skip_ref
  0.8 1.8 %mul.12 = bf16[4096,128]{1,0:T(8,128)(2,1)S(1)} multiply(bf16[4096,128]{1,0:T(8,128)(2,1)} %param.10, bf16[4096,128]{1,0:T(8,128)(2,1)} %param.11) | non-fusion elementwise | flops 524288 | bytes 3145728 | tf_op jit(solution)/shard_map/mul | solution.py:293
  2.6 0.0 copy-done.6
  2.6 0.2 pad_maximum_fusion
  2.8 0.0 copy-start.1
  2.8 0.0 copy-start.2
  2.8 0.0 copy-start.3
  2.8 0.0 copy-start.4
  2.9 55.8 %all_to_all.10.r_ref = bf16[32,256,128]{2,1,0:T(8,128)(2,1)S(1)} all-to-all(bf16[32,256,128]{2,1,0:T(8,128)(2,1)S(1)} %pad_maximum_fusion), channel_id=1, replica_groups=mesh['ctx'=8,'bit'=4] {'ctx','bit'}, dimensions={0} | all-to-all | bytes 4194304 | tf_op jit(solution)/shard_map/all_to_all | solution.py:300
  58.7 0.0 copy-done.1
  58.7 0.0 copy-done.2
  58.7 0.0 copy-done.3
  58.7 0.0 copy-done.4
  58.7 10.8 %shard_map.91 = bf16[32,128,128]{2,1,0:T(8,128)(2,1)S(1)} custom-call(bf16[32,256,128]{2,1,0:T(8,128)(2,1)S(1)} %all_to_all.10.r_ref, f32[1,128]{1,0:T(1,128)S(1)} %dynamic-slice_bitcast_fusion.skip_ref, bf16[768,256]{1,0:T(8,128)(2,1)S(1)} %copy-done.2, bf16[768,256]{1,0:T(8,128)(2,1)S(1)} %copy-done.1, f32[32,2,128]{2,1,0:T(2,128)S(1)} %copy-done.4, ...), custom_call_target="tpu_custom_call" | custom-call | flops 9663676416 | bytes 3145728 | tf_op jit(solution)/shard_map/pallas_call | solution.py:225
  69.5 0.0 copy-start.5
  69.5 29.7 %all_to_all.11 = bf16[32,128,128]{2,1,0:T(8,128)(2,1)S(1)} all-to-all(bf16[32,128,128]{2,1,0:T(8,128)(2,1)S(1)} %shard_map.91), channel_id=1, replica_groups=mesh['ctx'=8,'bit'=4] {'ctx','bit'}, dimensions={0} | all-to-all | bytes 2097152 | tf_op jit(solution)/shard_map/all_to_all | solution.py:305
  99.2 0.0 copy-done.5
  99.2 1.3 %fusion = bf16[4096,128]{1,0:T(8,128)(2,1)} fusion(bf16[4096,128]{1,0:T(8,128)(2,1)S(1)} %copy-done.5, bf16[32,128,128]{2,1,0:T(8,128)(2,1)S(1)} %all_to_all.11), kind=kLoop, calls=%fused_computation.2 | loop fusion | flops 2097152 | bytes 3145728 | tf_op jit(solution)/shard_map/convert_element_type | solution.py:306
Async XLA Ops:
  0.0 0.7 copy-start
  0.0 2.6 %copy-start.6 = (bf16[4096,128]{1,0:T(8,128)(2,1)S(1)}, bf16[4096,128]{1,0:T(8,128)(2,1)}, u32[]{:S(2)}) copy-start(bf16[4096,128]{1,0:T(8,128)(2,1)} %param.12) | copy-start | bytes 3145732
  2.8 55.9 %copy-start.1 = (bf16[768,256]{1,0:T(8,128)(2,1)S(1)}, bf16[768,256]{1,0:T(8,128)(2,1)}, u32[]{:S(2)}) copy-start(bf16[768,256]{1,0:T(8,128)(2,1)} %constant.26.clone.time_ref) | copy-start | bytes 1179652
  2.8 55.9 %copy-start.2 = (bf16[768,256]{1,0:T(8,128)(2,1)S(1)}, bf16[768,256]{1,0:T(8,128)(2,1)}, u32[]{:S(2)}) copy-start(bf16[768,256]{1,0:T(8,128)(2,1)} %constant.25.clone.freq_ref) | copy-start | bytes 1179652
  2.8 55.8 %copy-start.3 = (f32[32,2,128]{2,1,0:T(2,128)S(1)}, f32[32,2,128]{2,1,0:T(2,128)}, u32[]{:S(2)}) copy-start(f32[32,2,128]{2,1,0:T(2,128)} %constant.28.clone.tout_ref) | copy-start | bytes 98308
  2.8 55.8 %copy-start.4 = (f32[32,2,128]{2,1,0:T(2,128)S(1)}, f32[32,2,128]{2,1,0:T(2,128)}, u32[]{:S(2)}) copy-start(f32[32,2,128]{2,1,0:T(2,128)} %constant.27.clone.tin_ref) | copy-start | bytes 98308
  69.5 29.7 %copy-start.5 = (bf16[4096,128]{1,0:T(8,128)(2,1)S(1)}, bf16[4096,128]{1,0:T(8,128)(2,1)}, u32[]{:S(2)}) copy-start(bf16[4096,128]{1,0:T(8,128)(2,1)} %param.9) | copy-start | bytes 3145732

commit v2 on v1

--- a/solution.py
+++ b/solution.py
@@ -290,12 +290,12 @@
     axes = ("ctx", "bit")
     devices_all = lax.axis_size("ctx") * lax.axis_size("bit")
     ch_dev = channels // devices_all
-    products = key_proj * value_proj
+    products, gain = lax.optimization_barrier((key_proj * value_proj, skip_gain))
     send = jnp.concatenate(
         [filter_taps.reshape(devices_all, ch_dev, length), products.reshape(devices_all, ch_dev, length)], axis=1
     )
     mine = lax.axis_index(axes)
-    skip = lax.dynamic_slice(skip_gain, (mine * ch_dev,), (ch_dev,))[None, :]
+    skip = lax.dynamic_slice(gain, (mine * ch_dev,), (ch_dev,))[None, :]
     send, skip = lax.optimization_barrier((send, skip))
     recv = lax.all_to_all(send, axes, split_axis=0, concat_axis=0, tiled=True)
     if devices_all == 32 and length == 128 and ch_dev % 16 == 0:

time: 101 us -> 100 us (0.990)
  no operation moved by 1% of the time
where the time goes in v2:
time: 100 us; the launch traced here: 99.9 us
  blocking collectives  85.5 us (86%)
  Pallas kernels  10.8 us (11%)
  other arithmetic  3.36 us (3%)
    all_to_all x1, blocking collectives, on_device(): recv = lax.all_to_all(send, axes, split_axis=0, concat_axis=0, tiled=True)  55.8 us
    all_to_all x1, blocking collectives, on_device(): lax.all_to_all(mixed, axes, split_axis=0, concat_axis=0, tiled=True)  29.7 us
    pallas_call x1, Pallas kernels, conv_call(): pl.pallas_call(functools.partial(conv_kernel, group=group, ch=ch), out_sh...  10.8 us

profile of v2, /device:TPU:0, one launch (start us, length us, event | category | flops | bytes accessed | tf_op | source)
XLA Modules:
  0.0 99.9 jit_solution(9668755067591864720)
XLA Ops:
  0.0 0.0 copy-start
  0.0 0.0 copy-start.6
  0.0 1.9 %mul.12 = bf16[4096,128]{1,0:T(8,128)(2,1)S(1)} multiply(bf16[4096,128]{1,0:T(8,128)(2,1)} %param.10, bf16[4096,128]{1,0:T(8,128)(2,1)} %param.11) | non-fusion elementwise | flops 524288 | bytes 3145728 | tf_op jit(solution)/shard_map/mul | solution.py:293
  1.9 0.0 copy-done
  1.9 0.1 dynamic-slice_bitcast_fusion.skip_ref
  2.0 0.0 copy-done.6
  2.0 0.1 pad_maximum_fusion
  2.2 0.0 copy-start.1
  2.2 0.0 copy-start.2
  2.2 0.0 copy-start.3
  2.2 0.0 copy-start.4
  2.2 55.8 %all_to_all.10.r_ref = bf16[32,256,128]{2,1,0:T(8,128)(2,1)S(1)} all-to-all(bf16[32,256,128]{2,1,0:T(8,128)(2,1)S(1)} %pad_maximum_fusion), channel_id=1, replica_groups=mesh['ctx'=8,'bit'=4] {'ctx','bit'}, dimensions={0} | all-to-all | bytes 4194304 | tf_op jit(solution)/shard_map/all_to_all | solution.py:300
  58.0 0.0 copy-done.1
  58.0 0.0 copy-done.2
  58.0 0.0 copy-done.3
  58.0 0.0 copy-done.4
  58.0 10.8 %shard_map.91 = bf16[32,128,128]{2,1,0:T(8,128)(2,1)S(1)} custom-call(bf16[32,256,128]{2,1,0:T(8,128)(2,1)S(1)} %all_to_all.10.r_ref, f32[1,128]{1,0:T(1,128)S(1)} %dynamic-slice_bitcast_fusion.skip_ref, bf16[768,256]{1,0:T(8,128)(2,1)S(1)} %copy-done.2, bf16[768,256]{1,0:T(8,128)(2,1)S(1)} %copy-done.1, f32[32,2,128]{2,1,0:T(2,128)S(1)} %copy-done.4, ...), custom_call_target="tpu_custom_call" | custom-call | flops 9663676416 | bytes 3145728 | tf_op jit(solution)/shard_map/pallas_call | solution.py:225
  68.8 0.0 copy-start.5
  68.9 29.7 %all_to_all.11 = bf16[32,128,128]{2,1,0:T(8,128)(2,1)S(1)} all-to-all(bf16[32,128,128]{2,1,0:T(8,128)(2,1)S(1)} %shard_map.91), channel_id=1, replica_groups=mesh['ctx'=8,'bit'=4] {'ctx','bit'}, dimensions={0} | all-to-all | bytes 2097152 | tf_op jit(solution)/shard_map/all_to_all | solution.py:305
  98.6 0.0 copy-done.5
  98.6 1.3 %fusion = bf16[4096,128]{1,0:T(8,128)(2,1)} fusion(bf16[4096,128]{1,0:T(8,128)(2,1)S(1)} %copy-done.5, bf16[32,128,128]{2,1,0:T(8,128)(2,1)S(1)} %all_to_all.11), kind=kLoop, calls=%fused_computation.2 | loop fusion | flops 2097152 | bytes 3145728 | tf_op jit(solution)/shard_map/convert_element_type | solution.py:306
Async XLA Ops:
  0.0 1.9 %copy-start = (f32[4096]{0:T(1024)S(1)}, f32[4096]{0:T(1024)}, u32[]{:S(2)}) copy-start(f32[4096]{0:T(1024)} %param.13) | copy-start | bytes 49156
  0.0 2.0 %copy-start.6 = (bf16[4096,128]{1,0:T(8,128)(2,1)S(1)}, bf16[4096,128]{1,0:T(8,128)(2,1)}, u32[]{:S(2)}) copy-start(bf16[4096,128]{1,0:T(8,128)(2,1)} %param.12) | copy-start | bytes 3145732
  2.2 55.9 %copy-start.1 = (bf16[768,256]{1,0:T(8,128)(2,1)S(1)}, bf16[768,256]{1,0:T(8,128)(2,1)}, u32[]{:S(2)}) copy-start(bf16[768,256]{1,0:T(8,128)(2,1)} %constant.26.clone.time_ref) | copy-start | bytes 1179652
  2.2 55.9 %copy-start.2 = (bf16[768,256]{1,0:T(8,128)(2,1)S(1)}, bf16[768,256]{1,0:T(8,128)(2,1)}, u32[]{:S(2)}) copy-start(bf16[768,256]{1,0:T(8,128)(2,1)} %constant.25.clone.freq_ref) | copy-start | bytes 1179652
  2.2 55.8 %copy-start.3 = (f32[32,2,128]{2,1,0:T(2,128)S(1)}, f32[32,2,128]{2,1,0:T(2,128)}, u32[]{:S(2)}) copy-start(f32[32,2,128]{2,1,0:T(2,128)} %constant.28.clone.tout_ref) | copy-start | bytes 98308
  2.2 55.8 %copy-start.4 = (f32[32,2,128]{2,1,0:T(2,128)S(1)}, f32[32,2,128]{2,1,0:T(2,128)}, u32[]{:S(2)}) copy-start(f32[32,2,128]{2,1,0:T(2,128)} %constant.27.clone.tin_ref) | copy-start | bytes 98308
  68.8 29.7 %copy-start.5 = (bf16[4096,128]{1,0:T(8,128)(2,1)S(1)}, bf16[4096,128]{1,0:T(8,128)(2,1)}, u32[]{:S(2)}) copy-start(bf16[4096,128]{1,0:T(8,128)(2,1)} %param.9) | copy-start | bytes 3145732
